TPU v7x, 128 devices: a whole 4x4x4 slice. The times are simulated.
128 devices in a mesh: adapter: 32 (over y, x, core), mp: 4 (over z).
Axes of the slice: x: 4, y: 4, z: 4, core: 2. Of those that a mesh axis runs over, the one named last changes fastest.
Arguments:
- hidden: bfloat16 [8192, 4096], P('adapter', 'mp'), may hold values from -8 to 8
- subsets: int32 [8192, 8], P('adapter'), may hold values from 0 to 31, all different within a row; in each aligned block of 256 rows (0 to 255, 256 to 511, ...) at most 128 rows name the same one
- down_weight: bfloat16 [32, 4096, 256], P('adapter', 'mp'), may hold values from -0.09375 to 0.09375
- up_weight: bfloat16 [32, 256, 4096], P('adapter', None, 'mp'), may hold values from -0.375 to 0.375
- query_weight: bfloat16 [4096, 4096], P('mp'), may hold values from -0.08 to 2.08
- key_weight: bfloat16 [4096, 4096], P('mp'), may hold values from -0.08 to 2.08
Outputs:
- joined: bfloat16 [8192, 4096], P('adapter', 'mp')
Inputs may be any that keep to these rules, and one draw needn't show every extreme that they name: `subsets`: each row names 8 different adapters; within the rows of one index of the adapter axis no adapter is named by more than 128 rows.
All inputs are finite; a program needn't handle non-finite values.
Results may differ from a plain program's by a relative error of at most 0.025.
Values may be sent and summed in bfloat16 or wider, within the bound.
No kernel may reach another device: no remote copies, remote signals or barrier semaphores. Data moves between devices by JAX's collectives and lax.ppermute only.
A program may use at most 192 MiB of HBM per device.

v0:
```python
import jax
import jax.numpy as jnp
from jax import lax
from jax.sharding import PartitionSpec as P

D = 4096


def sent_to_all(x, axis):
    size = lax.axis_size(axis)
    return lax.all_to_all(jnp.broadcast_to(x[None], (size, *x.shape)), axis, 0, 0, tiled=True)


def over_copies(x, axis):
    return sent_to_all(x, axis).astype(jnp.float32).sum(axis=0)


def split_up(x, dim, size):
    before, after = (x.shape[:dim], x.shape[dim + 1 :])
    return jnp.moveaxis(x.reshape(*before, size, -1, *after), dim, 0)


def sent_and_summed(x, axis, dim):
    size = lax.axis_size(axis)
    parts = lax.all_to_all(split_up(x, dim, size), axis, 0, 0, tiled=True)
    return jnp.sum(parts.astype(jnp.float32), axis=0)


def in_order(parts, dim):
    parts = jnp.moveaxis(parts, 0, dim)
    shape = parts.shape
    return parts.reshape(*shape[:dim], shape[dim] * shape[dim + 1], *shape[dim + 2 :])


def collect(x, axis, dim):
    parts = sent_to_all(x, axis)
    return in_order(parts, dim)


def taken_together(x, axis):
    return sent_to_all(x, axis).sum(axis=0)


def tally(partial_sum):
    summed = over_copies(partial_sum.astype(jnp.bfloat16), "mp").astype(jnp.float32)
    return jnp.maximum(summed, 0.0).astype(jnp.bfloat16)


def per_device(hidden, subsets, down_weight, up_weight, query_weight, key_weight):
    row_count, width_local = hidden.shape
    fanout = subsets.shape[1]
    total_adapters = lax.axis_size("adapter") * down_weight.shape[0]
    capacity = min(row_count, 2 * row_count * fanout // total_adapters)
    labels = jnp.arange(total_adapters, dtype=jnp.int32)
    picks = (subsets[:, :, None] == labels[None, None, :]).astype(jnp.int32)
    chosen = jnp.sum(picks, axis=1)
    before = jnp.cumsum(chosen, axis=0) - chosen
    slot_rank = jnp.sum(picks * before[:, None, :], axis=2)
    flat_slot = subsets * capacity + slot_rank
    row_ids = jnp.broadcast_to(jnp.arange(row_count, dtype=jnp.int32)[:, None], flat_slot.shape)
    source_row = (
        jnp.zeros((total_adapters * capacity,), jnp.int32)
        .at[flat_slot.reshape(-1)]
        .set(row_ids.reshape(-1))
    )
    filled = jnp.zeros((total_adapters * capacity,), jnp.bool_).at[flat_slot.reshape(-1)].set(True)
    outgoing = jnp.where(
        filled[:, None], jnp.take(hidden, source_row, axis=0), jnp.zeros((), jnp.bfloat16)
    )
    outgoing = outgoing.reshape(total_adapters, capacity, width_local)
    query_part = jnp.dot(hidden, query_weight, preferred_element_type=jnp.float32)
    query_piece = sent_and_summed(query_part.astype(jnp.bfloat16), "mp", 1).astype(jnp.bfloat16)
    query = collect(query_piece, "mp", 1)
    probe = lax.dot_general(
        query, key_weight, (((1,), (1,)), ((), ())), preferred_element_type=jnp.float32
    ).astype(jnp.bfloat16)
    block = outgoing
    bottle = tally(
        jnp.einsum(
            "ncd,ndb->ncb",
            block,
            lax.all_gather(down_weight, "adapter", axis=0, tiled=True),
            preferred_element_type=jnp.float32,
        )
    )
    block = bottle
    returned = jnp.einsum(
        "ncb,nbd->ncd",
        block,
        lax.all_gather(up_weight, "adapter", axis=0, tiled=True),
        preferred_element_type=jnp.float32,
    ).astype(jnp.bfloat16)
    picked = jnp.take(returned.reshape(total_adapters * capacity, width_local), flat_slot, axis=0)
    widened = picked.astype(jnp.float32)
    base = hidden.astype(jnp.float32)
    probe_wide = probe.astype(jnp.float32)
    own_term = jnp.sum(base * probe_wide, axis=1)
    partial_logit = (
        jnp.einsum("rkd,rd->rk", widened, probe_wide, precision=lax.Precision.HIGHEST)
        + own_term[:, None]
    )
    logits = taken_together(partial_logit, "mp") * D ** (-0.5)
    share = jax.nn.softmax(logits, axis=-1)
    joined = base + jnp.einsum("rk,rkd->rd", share, widened, precision=lax.Precision.HIGHEST)
    return joined.astype(jnp.bfloat16)


def solution(mesh):
    return jax.shard_map(
        per_device,
        mesh=mesh,
        in_specs=(
            P("adapter", "mp"),
            P("adapter", None),
            P("adapter", "mp", None),
            P("adapter", None, "mp"),
            P("mp", None),
            P("mp", None),
        ),
        out_specs=P("adapter", "mp"),
        check_vma=False,
    )
```

profile of v0, /device:TPU:0, one launch (start us, length us, event | category | flops | bytes accessed | tf_op | source)
XLA Modules:
  0.0 257.7 jit_solution(9191249026218513655)
XLA Ops:
  6.5 0.0 all-gather.3.cloned.1.call-start
  6.5 0.7 all-gather.3.cloned.1.call-update
  7.3 0.0 all-gather.5.cloned.1.call-start
  7.3 0.7 all-gather.5.cloned.1.call-update
  8.0 5.9 %convolution_convert_fusion.1 = bf16[256,4096]{1,0:T(8,128)(2,1)S(1)} fusion(bf16[256,1024]{1,0:T(8,128)(2,1)} %param.6, bf16[1024,4096]{1,0:T(8,128)(2,1)} %param.10), kind=kOutput, calls=%fused_computation.11 | convolution fusion | flops 2148532224 | bytes 11010048 | tf_op jit(solution)/shard_map/dot_general | solution.py:71
  13.9 0.0 copy-start.1
  13.9 0.0 copy-start
  13.9 1.6 copy.58
  15.5 5.4 %all-to-all-start.1 = ((bf16[4,256,1024]{2,1,0:T(8,128)(2,1)}), bf16[4,256,1024]{2,1,0:T(8,128)(2,1)S(1)}, u32[]{:S(2)}, u32[]{:S(2)}) async-start(bf16[4,256,1024]{2,1,0:T(8,128)(2,1)} %bitcast.53), calls=%async_computation.1 | async-start | bytes 4194304 | tf_op jit(solution)/shard_map/all_to_all | solution.py:25
  20.9 0.0 copy-done.1
  21.0 0.6 reduce-window.6
  21.5 0.2 slice_reduce_fusion
  21.8 0.1 fusion.18
  21.9 0.1 select_reduce_fusion
  21.9 0.1 copy.39
  22.1 0.1 reshape.87
  22.2 0.1 reshape.120
  22.3 8.1 %scatter_custom_fusion.1 = s32[4096]{0:T(1024)S(1)} fusion(s32[2048]{0:T(1024)S(1)} %bitcast.55, s32[2048]{0:T(1024)S(1)} %reshape.120, s32[]{:T(128)} %constant.18.clone.1), kind=kCustom, calls=%fused_computation.45 | custom fusion | bytes 16388 | tf_op jit(solution)/shard_map/scatter | solution.py:64
  30.4 0.0 copy-done
  30.4 18.2 %gather_fusion = bf16[4096,1024]{1,0:T(8,128)(2,1)} fusion(bf16[256,1024]{1,0:T(8,128)(2,1)S(1)} %copy-done, s32[4096]{0:T(1024)S(1)} %fusion.19), kind=kCustom, calls=%fused_computation | custom fusion | bytes 16793600 | tf_op jit(solution)/shard_map/jit(_take)/gather | solution.py:68
  48.7 9.1 %scatter_custom_fusion = pred[4096]{0:T(1024)(128)(4,1)S(1)} fusion(s32[2048]{0:T(1024)S(1)} %bitcast.56, pred[2048]{0:T(1024)(128)(4,1)S(1)} %broadcast.50, pred[]{:T(512)} %constant.27.clone.1), kind=kCustom, calls=%fused_computation.48 | custom fusion | bytes 4097 | tf_op jit(solution)/shard_map/scatter | solution.py:66
  57.8 0.0 all-to-all-done.1
  57.8 0.4 reduce_sum.69
  58.2 0.2 copy.43
  58.4 1.4 broadcast_in_dim.97
  59.9 4.8 %all-to-all-start.2 = ((bf16[4,256,1024]{1,2,0:T(8,128)(2,1)}), bf16[4,256,1024]{1,2,0:T(8,128)(2,1)}, u32[]{:S(2)}, u32[]{:S(2)}) async-start(bf16[4,256,1024]{1,2,0:T(8,128)(2,1)} %broadcast_in_dim.97), calls=%async_computation.2 | async-start | bytes 4194304 | tf_op jit(solution)/shard_map/all_to_all | solution.py:11
  64.7 19.8 %all-gather.3.cloned.1.call-done = bf16[32,1024,256]{2,1,0:T(8,128)(2,1)} async-done(((bf16[1,1024,256]{2,1,0:T(8,128)(2,1)}), bf16[32,1024,256]{2,1,0:T(8,128)(2,1)}) %all-gather.3.cloned.1.call-update) | async-done | bytes 16777232 | tf_op jit(solution)/shard_map/all_gather | solution.py:82
  84.5 9.7 %fusion.12 = bf16[32,128,256]{2,1,0:T(8,128)(2,1)S(1)} fusion(bf16[32,1024,256]{2,1,0:T(8,128)(2,1)} %all-gather.3.cloned.1.call-done, bf16[32,128,1024]{2,1,0:T(8,128)(2,1)} %bitcast.52, pred[32,128]{1,0:T(8,128)(4,1)S(1)} %and_bitcast_fusion, pred[32,128]{1,0:T(8,128)(4,1)S(1)} %bitcast.57), kind=kOutput, calls=%fused_computation.22 | convolution fusion | flops 2156920832 | bytes 27271168 | tf_op jit(solution)/shard_map/ncd,ndb->ncb/dot_general | solution.py:79
  94.2 0.0 all-to-all-done.2
  94.2 4.3 %broadcast_in_dim.94 = bf16[4,32,128,256]{3,2,1,0:T(8,128)(2,1)} broadcast(bf16[32,128,256]{2,1,0:T(8,128)(2,1)S(1)} %fusion.12), dimensions={1,2,3} | broadcast | bytes 10485760 | tf_op jit(solution)/shard_map/broadcast_in_dim | solution.py:11
  98.4 5.8 %all-to-all-start = ((bf16[4,32,128,256]{3,2,1,0:T(8,128)(2,1)}), bf16[4,32,128,256]{3,2,1,0:T(8,128)(2,1)}, u32[]{:S(2)}, u32[]{:S(2)}) async-start(bf16[4,32,128,256]{3,2,1,0:T(8,128)(2,1)} %broadcast_in_dim.94), calls=%async_computation | async-start | bytes 16777216 | tf_op jit(solution)/shard_map/all_to_all | solution.py:11
  104.3 0.1 copy.40
  104.4 0.1 reshape.102
  104.5 0.2 copy.38
  104.7 6.5 %fusion.15 = (f32[256]{0:T(256)S(1)}, bf16[256,1024]{1,0:T(8,128)(2,1)S(1)}) fusion(bf16[256,1024]{1,0:T(8,128)(2,1)S(1)} %copy-done, bf16[256,4096]{0,1:T(8,128)(2,1)} %bitcast.10, bf16[1024,4096]{1,0:T(8,128)(2,1)} %param.11), kind=kOutput, calls=%fused_computation.26 | convolution fusion | flops 2148794112 | bytes 11535360 | tf_op jit(solution)/shard_map/dot_general | solution.py:74
  111.3 87.5 %all-to-all-done = bf16[4,32,128,256]{3,2,1,0:T(8,128)(2,1)} async-done(((bf16[4,32,128,256]{3,2,1,0:T(8,128)(2,1)}), bf16[4,32,128,256]{3,2,1,0:T(8,128)(2,1)}, u32[]{:S(2)}, u32[]{:S(2)}) %all-to-all-start) | async-done | bytes 8388640 | tf_op jit(solution)/shard_map/all_to_all | solution.py:11
  198.8 4.9 %convert_reduce_fusion = bf16[32,128,256]{2,1,0:T(8,128)(2,1)S(1)} fusion(bf16[4,32,128,256]{3,2,1,0:T(8,128)(2,1)} %all-to-all-done), kind=kLoop, calls=%fused_computation.4 | loop fusion | flops 7340032 | bytes 10485760 | tf_op jit(solution)/shard_map/reduce_sum | solution.py:15
  203.7 0.0 all-gather.5.cloned.1.call-done
  203.8 11.4 %convolution_convert_fusion = bf16[32,128,1024]{2,1,0:T(8,128)(2,1)} fusion(bf16[32,256,1024]{2,1,0:T(8,128)(2,1)} %all-gather.5.cloned.1.call-done, bf16[32,128,256]{2,1,0:T(8,128)(2,1)S(1)} %convert_reduce_fusion), kind=kOutput, calls=%fused_computation.10 | convolution fusion | flops 2154823680 | bytes 27262976 | tf_op jit(solution)/shard_map/ncb,nbd->ncd/dot_general | solution.py:87
  215.1 15.4 %gather_fusion.1 = bf16[2048,1024]{1,0:T(8,128)(2,1)} fusion(bf16[4096,1024]{1,0:T(8,128)(2,1)} %bitcast.51, s32[2048]{0:T(1024)S(1)} %broadcast_clamp_fusion), kind=kCustom, calls=%fused_computation.1 | custom fusion | bytes 8396800 | tf_op jit(solution)/shard_map/jit(_take)/gather | solution.py:93
  230.6 5.3 %fusion.8 = f32[256,1,8]{2,1,0:T(1,128)S(1)} fusion(bf16[2048,1024]{1,0:T(8,128)(2,1)} %gather_fusion.1, pred[256,8]{1,0:T(8,128)(4,1)S(1)} %copy.38, bf16[256,1024,1]{1,0,2:T(8,128)(2,1)S(1)} %bitcast.58), kind=kOutput, calls=%fused_computation.17 | convolution fusion | flops 6291456 | bytes 4728832 | tf_op jit(solution)/shard_map/rkd,rd->rk/dot_general | solution.py:99
  235.9 0.1 copy.45
  236.0 7.8 %all_to_all.20 = f32[4,256,8]{1,2,0:T(8,128)S(1)} all-to-all(f32[4,256,8]{1,2,0:T(8,128)S(1)} %broadcast_in_dim.98), channel_id=1, replica_groups=mesh['adapter'=32,'mp'=4] {'mp'}, dimensions={0} | all-to-all | bytes 65536 | tf_op jit(solution)/shard_map/all_to_all | solution.py:11
  243.8 0.1 copy.46
  244.0 5.8 %fusion.7 = f32[256,1,1024]{2,1,0:T(1,128)S(1)} fusion(f32[256,8,1]{1,2,0:T(1,128)S(1)} %copy.46, bf16[2048,1024]{1,0:T(8,128)(2,1)} %gather_fusion.1, pred[256,8]{1,0:T(8,128)(4,1)S(1)} %copy.38), kind=kOutput, calls=%fused_computation.16 | convolution fusion | flops 27262976 | bytes 5253120 | tf_op jit(solution)/shard_map/rk,rkd->rd/dot_general | solution.py:104
  249.8 1.1 fusion.16
  (18 shorter events, 0.2 us)
Async XLA Ops:
  6.5 77.9 %all-gather.3.cloned.1.call-start = ((), (), s32[]{:S(2)}) async-start(), calls=%async_computation.4 | async-start | bytes 17301504 | tf_op jit(solution)/shard_map/all_gather | solution.py:82
  7.3 196.5 %all-gather.5.cloned.1.call-start = ((), (), s32[]{:S(2)}) async-start(), calls=%async_computation.5 | async-start | bytes 17301504 | tf_op jit(solution)/shard_map/all_gather | solution.py:90
  13.9 7.0 %copy-start.1 = (s32[256,8]{0,1:T(8,128)S(1)}, s32[256,8]{0,1:T(8,128)}, u32[]{:S(2)}) copy-start(s32[256,8]{0,1:T(8,128)} %param.7) | copy-start | bytes 24580
  13.9 16.5 %copy-start = (bf16[256,1024]{1,0:T(8,128)(2,1)S(1)}, bf16[256,1024]{1,0:T(8,128)(2,1)}, u32[]{:S(2)}) copy-start(bf16[256,1024]{1,0:T(8,128)(2,1)} %param.6) | copy-start | bytes 1572868
  15.5 42.3 %all-to-all-start.1 = ((bf16[4,256,1024]{2,1,0:T(8,128)(2,1)}), bf16[4,256,1024]{2,1,0:T(8,128)(2,1)S(1)}, u32[]{:S(2)}, u32[]{:S(2)}) async-start(bf16[4,256,1024]{2,1,0:T(8,128)(2,1)} %bitcast.53), calls=%async_computation.1 | async-start | bytes 4194304 | tf_op jit(solution)/shard_map/all_to_all | solution.py:25
  59.9 34.3 %all-to-all-start.2 = ((bf16[4,256,1024]{1,2,0:T(8,128)(2,1)}), bf16[4,256,1024]{1,2,0:T(8,128)(2,1)}, u32[]{:S(2)}, u32[]{:S(2)}) async-start(bf16[4,256,1024]{1,2,0:T(8,128)(2,1)} %broadcast_in_dim.97), calls=%async_computation.2 | async-start | bytes 4194304 | tf_op jit(solution)/shard_map/all_to_all | solution.py:11
  98.4 100.4 %all-to-all-start = ((bf16[4,32,128,256]{3,2,1,0:T(8,128)(2,1)}), bf16[4,32,128,256]{3,2,1,0:T(8,128)(2,1)}, u32[]{:S(2)}, u32[]{:S(2)}) async-start(bf16[4,32,128,256]{3,2,1,0:T(8,128)(2,1)} %broadcast_in_dim.94), calls=%async_computation | async-start | bytes 16777216 | tf_op jit(solution)/shard_map/all_to_all | solution.py:11
Sparse Core Ops, SparseCore 0:
  9.6 74.8 all-gather.2
  86.7 71.8 all-gather.4
where the time goes:
time: 258 us
  waiting for transfers between devices  109 us (42%)
  local copies, waits for them, and re-layouts  59.5 us (23%)
  matrix products  44.6 us (17%)
  starting transfers between devices  16.1 us (6%)
  between operations  13.6 us (5%)
  blocking collectives  7.81 us (3%)
  other arithmetic  7.31 us (3%)
    all_to_all x2, waiting for transfers between devices, sent_to_all(): lax.all_to_all(jnp.broadcast_to(x[None], (size, *x.shape)), axis, 0, 0, t...  87.5 us
    all_gather x1, waiting for transfers between devices, per_device(): lax.all_gather(down_weight, 'adapter', axis=0, tiled=True)  19.8 us
    gather x1, local copies, waits for them, and re-layouts, per_device(): jnp.take(hidden, source_row, axis=0)  18.2 us
    gather x1, local copies, waits for them, and re-layouts, per_device(): jnp.take(returned.reshape(total_adapters * capacity, width_local), flat_s...  15.4 us
    dot_general x1, matrix products, per_device(): jnp.einsum('ncb,nbd->ncd', block, lax.all_gather(up_weight, 'adapter', ax...  11.4 us
    all_to_all x2, starting transfers between devices, sent_to_all(): lax.all_to_all(jnp.broadcast_to(x[None], (size, *x.shape)), axis, 0, 0, t...  10.6 us
    dot_general x1, matrix products, per_device(): jnp.einsum('ncd,ndb->ncb', block, lax.all_gather(down_weight, 'adapter',...  9.7 us
    scatter x1, local copies, waits for them, and re-layouts, per_device(): jnp.zeros((total_adapters * capacity,), jnp.bool_).at[flat_slot.reshape(-1)]  9.12 us
  transfers between devices with their start and end apart: 5, of which 2 were waited for; matrix products, arithmetic and copies ran while one was open for 28% of the time, Pallas kernels for 0%

commit v1 on v0

--- a/solution.py
+++ b/solution.py
@@ -1,9 +1,21 @@
+import functools
 import jax
 import jax.numpy as jnp
 from jax import lax
 from jax.sharding import PartitionSpec as P
+from jax.lax import all_to_all, axis_size
 
 D = 4096
+
+
+def pack_pieces_all(view, mesh_ax):
+    how_many = axis_size(mesh_ax)
+    pile = list(map(lambda dev_i: how_many if dev_i == 0 else 1, range(view.ndim)))
+    prior = all_to_all(jnp.tile(view, pile), mesh_ax, split_axis=0, concat_axis=0, tiled=True)
+    return prior
+
+
+regions_manage = functools.partial(pack_pieces_all, mesh_ax="adapter")
 
 
 def sent_to_all(x, axis):
@@ -77,10 +89,7 @@
     block = outgoing
     bottle = tally(
         jnp.einsum(
-            "ncd,ndb->ncb",
-            block,
-            lax.all_gather(down_weight, "adapter", axis=0, tiled=True),
-            preferred_element_type=jnp.float32,
+            "ncd,ndb->ncb", block, regions_manage(down_weight), preferred_element_type=jnp.float32
         )
     )
     block = bottle

time: 258 us -> 479 us (1.86)
  the two profiles are of different devices: /device:TPU:0 before, /device:TPU:28 now
where the time goes in v1:
time: 479 us; the launch traced here: 478 us
  waiting for transfers between devices  291 us (61%)
  local copies, waits for them, and re-layouts  64.6 us (13%)
  matrix products  44.5 us (9%)
  blocking collectives  39.2 us (8%)
  starting transfers between devices  17.9 us (4%)
  between operations  13.7 us (3%)
  other arithmetic  7.31 us (2%)
    all_to_all x1, waiting for transfers between devices, pack_pieces_all(): all_to_all(jnp.tile(view, pile), mesh_ax, split_axis=0, concat_axis=0, ti...  187 us
    all_to_all x2, waiting for transfers between devices, sent_to_all(): lax.all_to_all(jnp.broadcast_to(x[None], (size, *x.shape)), axis, 0, 0, t...  103 us
    all_to_all x1, blocking collectives, sent_and_summed(): parts = lax.all_to_all(split_up(x, dim, size), axis, 0, 0, tiled=True)  31.4 us
    gather x1, local copies, waits for them, and re-layouts, per_device(): jnp.take(hidden, source_row, axis=0)  18.2 us
    gather x1, local copies, waits for them, and re-layouts, per_device(): jnp.take(returned.reshape(total_adapters * capacity, width_local), flat_s...  15.4 us
    dot_general x1, matrix products, per_device(): jnp.einsum('ncb,nbd->ncd', block, lax.all_gather(up_weight, 'adapter', ax...  11.4 us
    all_to_all x2, starting transfers between devices, sent_to_all(): lax.all_to_all(jnp.broadcast_to(x[None], (size, *x.shape)), axis, 0, 0, t...  10.3 us
    dot_general x1, matrix products, per_device(): jnp.einsum('ncd,ndb->ncb', block, regions_manage(down_weight), preferred_...  9.72 us
  transfers between devices with their start and end apart: 4, of which 3 were waited for; matrix products, arithmetic and copies ran while one was open for 16% of the time, Pallas kernels for 0%

profile of v1, /device:TPU:28, one launch (start us, length us, event | category | flops | bytes accessed | tf_op | source)
XLA Modules:
  0.0 478.0 jit_solution(7472549547056646404)
XLA Ops:
  6.5 0.0 all-gather.2.cloned.1.call-start
  6.5 0.7 all-gather.2.cloned.1.call-update
  7.3 5.9 %convolution_convert_fusion.1 = bf16[256,4096]{1,0:T(8,128)(2,1)S(1)} fusion(bf16[256,1024]{1,0:T(8,128)(2,1)} %param.6, bf16[1024,4096]{1,0:T(8,128)(2,1)} %param.10), kind=kOutput, calls=%fused_computation.11 | convolution fusion | flops 2148532224 | bytes 11010048 | tf_op jit(solution)/shard_map/dot_general | solution.py:83
  13.2 0.0 copy-start.1
  13.2 0.2 copy.58
  13.4 31.4 %all_to_all.25 = bf16[4,256,1024]{2,1,0:T(8,128)(2,1)S(1)} all-to-all(bf16[4,256,1024]{2,1,0:T(8,128)(2,1)S(1)} %bitcast.54), channel_id=1, replica_groups=mesh['adapter'=32,'mp'=4] {'mp'}, dimensions={0} | all-to-all | bytes 4194304 | tf_op jit(solution)/shard_map/all_to_all | solution.py:37
  44.8 0.0 copy-done.1
  44.8 6.5 %tile.10 = bf16[32,1024,256]{2,1,0:T(8,128)(2,1)} broadcast(bf16[1024,256]{1,0:T(8,128)(2,1)S(1)} %bitcast.56), dimensions={1,2} | broadcast | bytes 17301504 | tf_op jit(solution)/shard_map/tile | solution.py:14
  51.2 0.0 copy-start.2
  51.3 7.6 %all-to-all-start = ((bf16[32,1024,256]{2,1,0:T(8,128)(2,1)}), bf16[32,1024,256]{2,1,0:T(8,128)(2,1)}, u32[]{:S(2)}, u32[]{:S(2)}) async-start(bf16[32,1024,256]{2,1,0:T(8,128)(2,1)} %tile.10), calls=%async_computation | async-start | bytes 33554432 | tf_op jit(solution)/shard_map/all_to_all | solution.py:14
  58.8 0.0 copy-done.2
  58.9 0.0 copy-start
  58.9 0.6 reduce-window.6
  59.5 0.2 slice_reduce_fusion
  59.7 0.1 fusion.18
  59.8 0.1 select_reduce_fusion
  59.9 0.1 copy.39
  60.0 0.1 reshape.90
  60.2 0.1 reshape.123
  60.3 8.1 %scatter_custom_fusion.1 = s32[4096]{0:T(1024)S(1)} fusion(s32[2048]{0:T(1024)S(1)} %bitcast.57, s32[2048]{0:T(1024)S(1)} %reshape.123, s32[]{:T(128)} %constant.18.clone.1), kind=kCustom, calls=%fused_computation.45 | custom fusion | bytes 16388 | tf_op jit(solution)/shard_map/scatter | solution.py:76
  68.4 0.0 copy-done
  68.4 18.2 %gather_fusion = bf16[4096,1024]{1,0:T(8,128)(2,1)} fusion(bf16[256,1024]{1,0:T(8,128)(2,1)S(1)} %copy-done, s32[4096]{0:T(1024)S(1)} %fusion.19), kind=kCustom, calls=%fused_computation | custom fusion | bytes 16793600 | tf_op jit(solution)/shard_map/jit(_take)/gather | solution.py:80
  86.6 9.1 %scatter_custom_fusion = pred[4096]{0:T(1024)(128)(4,1)S(1)} fusion(s32[2048]{0:T(1024)S(1)} %bitcast.58, pred[2048]{0:T(1024)(128)(4,1)S(1)} %broadcast.52, pred[]{:T(512)} %constant.27.clone.1), kind=kCustom, calls=%fused_computation.48 | custom fusion | bytes 4097 | tf_op jit(solution)/shard_map/scatter | solution.py:78
  95.7 0.4 reduce_sum.69
  96.2 0.2 copy.43
  96.4 187.0 %all-to-all-done = bf16[32,1024,256]{2,1,0:T(8,128)(2,1)} async-done(((bf16[32,1024,256]{2,1,0:T(8,128)(2,1)}), bf16[32,1024,256]{2,1,0:T(8,128)(2,1)}, u32[]{:S(2)}, u32[]{:S(2)}) %all-to-all-start) | async-done | bytes 16777248 | tf_op jit(solution)/shard_map/all_to_all | solution.py:14
  283.4 1.5 broadcast_in_dim.97
  284.9 4.6 all-to-all-start.3
  289.5 9.7 %fusion.12 = bf16[32,128,256]{2,1,0:T(8,128)(2,1)S(1)} fusion(bf16[32,1024,256]{2,1,0:T(8,128)(2,1)} %all-to-all-done, bf16[32,128,1024]{2,1,0:T(8,128)(2,1)} %bitcast.53, pred[32,128]{1,0:T(8,128)(4,1)S(1)} %and_bitcast_fusion, pred[32,128]{1,0:T(8,128)(4,1)S(1)} %bitcast.59), kind=kOutput, calls=%fused_computation.22 | convolution fusion | flops 2156920832 | bytes 27271168 | tf_op jit(solution)/shard_map/ncd,ndb->ncb/dot_general | solution.py:91
  299.2 17.1 %all-to-all-done.3 = bf16[4,256,1024]{1,2,0:T(8,128)(2,1)} async-done(((bf16[4,256,1024]{1,2,0:T(8,128)(2,1)}), bf16[4,256,1024]{1,2,0:T(8,128)(2,1)}, u32[]{:S(2)}, u32[]{:S(2)}) %all-to-all-start.3) | async-done | bytes 2097184 | tf_op jit(solution)/shard_map/all_to_all | solution.py:23
  316.4 4.3 broadcast_in_dim.94
  320.6 5.7 %all-to-all-start.1 = ((bf16[4,32,128,256]{3,2,1,0:T(8,128)(2,1)}), bf16[4,32,128,256]{3,2,1,0:T(8,128)(2,1)}, u32[]{:S(2)}, u32[]{:S(2)}) async-start(bf16[4,32,128,256]{3,2,1,0:T(8,128)(2,1)} %broadcast_in_dim.94), calls=%async_computation.1 | async-start | bytes 16777216 | tf_op jit(solution)/shard_map/all_to_all | solution.py:23
  326.3 0.1 copy.40
  326.4 0.1 reshape.105
  326.5 0.2 copy.38
  326.7 6.5 %fusion.15 = (f32[256]{0:T(256)S(1)}, bf16[256,1024]{1,0:T(8,128)(2,1)S(1)}) fusion(bf16[256,1024]{1,0:T(8,128)(2,1)S(1)} %copy-done, bf16[256,4096]{0,1:T(8,128)(2,1)} %bitcast.11, bf16[1024,4096]{1,0:T(8,128)(2,1)} %param.11), kind=kOutput, calls=%fused_computation.26 | convolution fusion | flops 2148794112 | bytes 11535360 | tf_op jit(solution)/shard_map/dot_general | solution.py:86
  333.2 86.0 %all-to-all-done.1 = bf16[4,32,128,256]{3,2,1,0:T(8,128)(2,1)} async-done(((bf16[4,32,128,256]{3,2,1,0:T(8,128)(2,1)}), bf16[4,32,128,256]{3,2,1,0:T(8,128)(2,1)}, u32[]{:S(2)}, u32[]{:S(2)}) %all-to-all-start.1) | async-done | bytes 8388640 | tf_op jit(solution)/shard_map/all_to_all | solution.py:23
  419.2 4.9 %convert_reduce_fusion = bf16[32,128,256]{2,1,0:T(8,128)(2,1)S(1)} fusion(bf16[4,32,128,256]{3,2,1,0:T(8,128)(2,1)} %all-to-all-done.1), kind=kLoop, calls=%fused_computation.4 | loop fusion | flops 7340032 | bytes 10485760 | tf_op jit(solution)/shard_map/reduce_sum | solution.py:27
  424.1 0.0 all-gather.2.cloned.1.call-done
  424.1 11.4 %convolution_convert_fusion = bf16[32,128,1024]{2,1,0:T(8,128)(2,1)} fusion(bf16[32,256,1024]{2,1,0:T(8,128)(2,1)} %all-gather.2.cloned.1.call-done, bf16[32,128,256]{2,1,0:T(8,128)(2,1)S(1)} %convert_reduce_fusion), kind=kOutput, calls=%fused_computation.10 | convolution fusion | flops 2154823680 | bytes 27262976 | tf_op jit(solution)/shard_map/ncb,nbd->ncd/dot_general | solution.py:96
  435.5 15.4 %gather_fusion.1 = bf16[2048,1024]{1,0:T(8,128)(2,1)} fusion(bf16[4096,1024]{1,0:T(8,128)(2,1)} %bitcast.52, s32[2048]{0:T(1024)S(1)} %broadcast_clamp_fusion), kind=kCustom, calls=%fused_computation.1 | custom fusion | bytes 8396800 | tf_op jit(solution)/shard_map/jit(_take)/gather | solution.py:102
  450.9 5.3 %fusion.8 = f32[256,1,8]{2,1,0:T(1,128)S(1)} fusion(bf16[2048,1024]{1,0:T(8,128)(2,1)} %gather_fusion.1, pred[256,8]{1,0:T(8,128)(4,1)S(1)} %copy.38, bf16[256,1024,1]{1,0,2:T(8,128)(2,1)S(1)} %bitcast.60), kind=kOutput, calls=%fused_computation.17 | convolution fusion | flops 6291456 | bytes 4728832 | tf_op jit(solution)/shard_map/rkd,rd->rk/dot_general | solution.py:108
  456.2 0.1 copy.45
  456.3 7.8 %all_to_all.26 = f32[4,256,8]{1,2,0:T(8,128)S(1)} all-to-all(f32[4,256,8]{1,2,0:T(8,128)S(1)} %broadcast_in_dim.98), channel_id=1, replica_groups=mesh['adapter'=32,'mp'=4] {'mp'}, dimensions={0} | all-to-all | bytes 65536 | tf_op jit(solution)/shard_map/all_to_all | solution.py:23
  464.2 0.1 copy.46
  464.3 5.8 %fusion.7 = f32[256,1,1024]{2,1,0:T(1,128)S(1)} fusion(f32[256,8,1]{1,2,0:T(1,128)S(1)} %copy.46, bf16[2048,1024]{1,0:T(8,128)(2,1)} %gather_fusion.1, pred[256,8]{1,0:T(8,128)(4,1)S(1)} %copy.38), kind=kOutput, calls=%fused_computation.16 | convolution fusion | flops 27262976 | bytes 5253120 | tf_op jit(solution)/shard_map/rk,rkd->rd/dot_general | solution.py:113
  470.1 1.1 fusion.16
  (18 shorter events, 0.2 us)
Async XLA Ops:
  6.5 417.6 %all-gather.2.cloned.1.call-start = ((), (), s32[]{:S(2)}) async-start(), calls=%async_computation.5 | async-start | bytes 17301504 | tf_op jit(solution)/shard_map/all_gather | solution.py:99
  13.2 31.6 %copy-start.1 = (bf16[1,1024,256]{2,1,0:T(8,128)(2,1)S(1)}, bf16[1,1024,256]{2,1,0:T(8,128)(2,1)}, u32[]{:S(2)}) copy-start(bf16[1,1024,256]{2,1,0:T(8,128)(2,1)} %param.8) | copy-start | bytes 1572868
  51.2 7.6 %copy-start.2 = (s32[256,8]{0,1:T(8,128)S(1)}, s32[256,8]{0,1:T(8,128)}, u32[]{:S(2)}) copy-start(s32[256,8]{0,1:T(8,128)} %param.7) | copy-start | bytes 24580
  51.3 232.1 %all-to-all-start = ((bf16[32,1024,256]{2,1,0:T(8,128)(2,1)}), bf16[32,1024,256]{2,1,0:T(8,128)(2,1)}, u32[]{:S(2)}, u32[]{:S(2)}) async-start(bf16[32,1024,256]{2,1,0:T(8,128)(2,1)} %tile.10), calls=%async_computation | async-start | bytes 33554432 | tf_op jit(solution)/shard_map/all_to_all | solution.py:14
  58.9 9.5 %copy-start = (bf16[256,1024]{1,0:T(8,128)(2,1)S(1)}, bf16[256,1024]{1,0:T(8,128)(2,1)}, u32[]{:S(2)}) copy-start(bf16[256,1024]{1,0:T(8,128)(2,1)} %param.6) | copy-start | bytes 1572868
  284.9 31.5 %all-to-all-start.3 = ((bf16[4,256,1024]{1,2,0:T(8,128)(2,1)}), bf16[4,256,1024]{1,2,0:T(8,128)(2,1)}, u32[]{:S(2)}, u32[]{:S(2)}) async-start(bf16[4,256,1024]{1,2,0:T(8,128)(2,1)} %broadcast_in_dim.97), calls=%async_computation.3 | async-start | bytes 4194304 | tf_op jit(solution)/shard_map/all_to_all | solution.py:23
  320.6 98.6 %all-to-all-start.1 = ((bf16[4,32,128,256]{3,2,1,0:T(8,128)(2,1)}), bf16[4,32,128,256]{3,2,1,0:T(8,128)(2,1)}, u32[]{:S(2)}, u32[]{:S(2)}) async-start(bf16[4,32,128,256]{3,2,1,0:T(8,128)(2,1)} %broadcast_in_dim.94), calls=%async_computation.1 | async-start | bytes 16777216 | tf_op jit(solution)/shard_map/all_to_all | solution.py:23
Sparse Core Ops, SparseCore 0:
  9.6 194.5 all-gather.1
